TPU v7x, 32 devices: a whole 2x2x4 slice. The times are simulated.
32 devices in a mesh: seq: 8 (over z, x), vocab: 4 (over y, core).
Axes of the slice: x: 2, y: 2, z: 4, core: 2. Of those that a mesh axis runs over, the one named last changes fastest.
Arguments:
- hidden: bfloat16 [2, 1024, 2048], P(None, 'seq'), may hold values from -6 to 6
- embedded: bfloat16 [2, 1024, 2048], P(None, 'seq'), may hold values from -6 to 6
- targets: int32 [2, 1024], P(None, 'seq'), may hold values from 0 to 51199
- main_mask: int32 [2, 1024], P(None, 'seq'), may hold values 0 or 1
- mtp_mask: int32 [2, 1024], P(None, 'seq'), may hold values from 0 to 1, as said below
- lengths: int32 [2], replicated, may hold values from 256 to 1024, as said below
- head_weight: bfloat16 [2048, 51200], P(None, ('seq', 'vocab')), may hold values from -7.6733202 to 7.6733202
- projection: bfloat16 [4096, 2048], P(None, 'vocab'), may hold values from -0.09375 to 0.09375
- main_gain: float32 [2048], replicated, may hold values from 0.5 to 1.5
- hidden_gain: float32 [2048], replicated, may hold values from 0.5 to 1.5
- embed_gain: float32 [2048], replicated, may hold values from 0.5 to 1.5
- mtp_gain: float32 [2048], replicated, may hold values from 0.5 to 1.5
Outputs:
- main_tokens: float32 [2, 1024], P(None, 'seq')
- mtp_tokens: float32 [2, 1024], P(None, 'seq')
- total_loss: float32 [], replicated
Inputs may be any that keep to these rules, and one draw needn't show every extreme that they name: `mtp_mask`: 1 at every position that is a multiple of 128. `lengths`: the first sequence has length 1024.
All inputs are finite; a program needn't handle non-finite values. No bound on the sum of `main_mask` on one device may be relied on, other than what follows from the above.
Results may differ from a plain program's by a relative error of at most 0.0004.
The roundings to bfloat16 on the way count: a program that leaves them out, or rounds other values in their place, can miss the bound.
Values may be sent and summed in bfloat16 or wider, within the bound.
A program may use at most 128 MiB of HBM per device.

v0:
```python
import jax
import jax.numpy as jnp
from jax import lax
from jax.sharding import PartitionSpec as P

EPSILON = 1e-06
MTP_WEIGHT = 0.3


def from_behind(block, axis, distance):
    devices = range(lax.axis_size(axis))
    route = [(i - distance, i) for i in devices if i - distance in devices]
    return lax.ppermute(block, axis, route)


def partner_2(value, axis, apart):
    mask = 2**apart
    pairs = [(source, source ^ mask) for source in range(lax.axis_size(axis))]
    return lax.ppermute(value, axis, pairs)


def normalize(values, gain_vec):
    values = values.astype(jnp.float32)
    mean_square = jnp.mean(values * values, axis=-1, keepdims=True)
    return values * lax.rsqrt(mean_square + EPSILON) * gain_vec


def column_stats(logits, column_ids, wanted):
    highest = jnp.max(logits, axis=1)
    exp_total = jnp.sum(jnp.exp(logits - highest[:, None]), axis=1)
    picked = jnp.sum(jnp.where(column_ids[None, :] == wanted[:, None], logits, 0.0), axis=1)
    return (highest, exp_total, picked)


def join_stats(earlier, latter):
    highest = jnp.maximum(earlier[0], latter[0])
    exp_total = earlier[1] * jnp.exp(earlier[0] - highest) + latter[1] * jnp.exp(
        latter[0] - highest
    )
    return (highest, exp_total, earlier[2] + latter[2])


def shards(
    hidden,
    embedded,
    targets,
    main_mask,
    mtp_mask,
    lengths,
    head_weight,
    projection,
    main_gain,
    hidden_gain,
    embed_gain,
    mtp_gain,
):
    batches, seq_len, model_width = hidden.shape
    seq_index = lax.axis_index("seq")
    vocab_index = lax.axis_index("vocab")
    vocab_count = lax.axis_size("vocab")
    block_cols = head_weight.shape[1]
    positions = seq_index * seq_len + lax.broadcasted_iota(jnp.int32, (batches, seq_len), 1)
    length_col = lengths[:, None]
    keep_main = ((main_mask == 1) & (positions + 1 < length_col)).astype(jnp.float32)
    keep_mtp = ((mtp_mask == 1) & (positions >= 1) & (positions + 1 < length_col)).astype(
        jnp.float32
    )
    count_main = jnp.sum(keep_main)
    count_mtp = jnp.sum(keep_mtp)
    counted = lax.psum((count_main, count_mtp), "seq")
    main_rows = normalize(hidden, main_gain).astype(jnp.bfloat16).reshape(-1, model_width)
    incoming = from_behind(hidden[:, seq_len - 1 :, :], "seq", 1)
    previous = jnp.concatenate([incoming, hidden[:, : seq_len - 1, :]], axis=1)
    joined = jnp.concatenate(
        [normalize(previous, hidden_gain), normalize(embedded, embed_gain)], axis=2
    )
    joined = joined.astype(jnp.bfloat16).reshape(-1, 2 * model_width)
    partial_value = jnp.dot(joined, projection, preferred_element_type=jnp.float32).astype(
        jnp.bfloat16
    )
    mixed = lax.all_gather(partial_value, "vocab", axis=1, tiled=True)
    mtp_rows = normalize(mixed, mtp_gain).astype(jnp.bfloat16)
    all_rows = jnp.concatenate([main_rows, mtp_rows], axis=0)
    flat_targets = targets.reshape(-1)
    wanted = jnp.concatenate([flat_targets, flat_targets], axis=0)
    held_cols = head_weight
    levels = lax.axis_size("seq").bit_length() - 1
    for bit_number in range(1, levels):
        received = partner_2(held_cols, "seq", bit_number)
        upper_half = seq_index >> bit_number & 1 == 1
        held_cols = jnp.where(
            upper_half,
            jnp.concatenate([received, held_cols], axis=1),
            jnp.concatenate([held_cols, received], axis=1),
        )
    partner = partner_2(all_rows, "seq", 0)
    partner_wanted = partner_2(wanted, "seq", 0)
    column_pos = lax.broadcasted_iota(jnp.int32, (held_cols.shape[1],), 0)
    anchor_seq = (seq_index & 1) + 2 * (column_pos // block_cols)
    column_ids = (anchor_seq * vocab_count + vocab_index) * block_cols + column_pos % block_cols
    logits = jnp.dot(
        jnp.concatenate([all_rows, partner], axis=0), held_cols, preferred_element_type=jnp.float32
    )
    row_count = all_rows.shape[0]
    own_stats = column_stats(logits[:row_count], column_ids, wanted)
    peer_stats = column_stats(logits[row_count:], column_ids, partner_wanted)
    returned = partner_2((peer_stats[0], peer_stats[1], peer_stats[2]), "seq", 0)
    highest, exp_total, picked = join_stats(own_stats, returned)
    global_max = lax.pmax(highest, "vocab")
    global_total, target_logit = lax.psum(
        (exp_total * jnp.exp(highest - global_max), picked), "vocab"
    )
    losses = global_max + jnp.log(global_total) - target_logit
    half_rows = batches * seq_len
    main_tokens = keep_main * losses[:half_rows].reshape(batches, seq_len)
    mtp_tokens = keep_mtp * losses[half_rows:].reshape(batches, seq_len)
    main_sum = jnp.sum(main_tokens)
    mtp_sum = jnp.sum(mtp_tokens)
    summed = lax.psum((main_sum, mtp_sum), "seq")
    total_main, total_mtp = summed
    kept_main, kept_mtp = counted
    total_loss = total_main / jnp.maximum(kept_main, 1.0) + MTP_WEIGHT * total_mtp / jnp.maximum(
        kept_mtp, 1.0
    )
    return (main_tokens, mtp_tokens, total_loss)


def solution(mesh):
    return jax.shard_map(
        shards,
        mesh=mesh,
        in_specs=(
            P(None, "seq", None),
            P(None, "seq", None),
            P(None, "seq"),
            P(None, "seq"),
            P(None, "seq"),
            P(),
            P(None, ("seq", "vocab")),
            P(None, "vocab"),
            P(),
            P(),
            P(),
            P(),
        ),
        out_specs=(P(None, "seq"), P(None, "seq"), P()),
        check_vma=False,
    )
```

profile of v0, /device:TPU:0, one launch (start us, length us, event | category | flops | bytes accessed | tf_op | source)
XLA Modules:
  0.0 926.5 jit_solution(852602479931637078)
XLA Ops:
  7.2 0.0 all-gather.2.cloned.1.call-start
  7.2 3.1 collective-permute-start.2
  10.3 0.0 copy-start.1
  10.3 0.0 copy-start.2
  10.3 0.0 copy-start.3
  10.3 141.4 %collective-permute-done.2 = bf16[2048,1600]{0,1:T(8,128)(2,1)} collective-permute-done((bf16[2048,1600]{0,1:T(8,128)(2,1)}, bf16[2048,1600]{0,1:T(8,128)(2,1)}, u32[]{:S(2)}, u32[]{:S(2)}) %collective-permute-start.2) | collective-permute-done | bytes 6553632 | tf_op jit(solution)/shard_map/ppermute | solution.py:19
  151.8 15.6 %maximum_select_fusion.2 = bf16[2048,3200]{0,1:T(8,128)(2,1)} fusion(bf16[2048,1600]{0,1:T(8,128)(2,1)} %param.18, bf16[2048,1600]{0,1:T(8,128)(2,1)} %collective-permute-done.2, pred[]{:T(512)S(6)} %eq.40), kind=kLoop, calls=%fused_computation.8 | loop fusion | flops 58982400 | bytes 26214400 | tf_op jit(solution)/shard_map/jit(_where)/select_n | solution.py:91
  167.4 0.0 copy-start.4
  167.4 0.0 copy-start.11
  167.4 2.8 collective-permute-start.3
  170.2 0.0 copy-done.1
  170.2 3.4 collective-permute-start
  173.7 0.0 copy-done.2
  173.7 0.3 fusion.15
  174.0 0.0 copy-done.3
  174.0 0.3 fusion.17
  174.3 0.8 collective-permute-done
  175.1 0.4 multiply_reduce_fusion
  175.5 0.3 maximum_convert_fusion
  175.8 0.0 copy-done.4
  175.9 0.0 copy-start.5
  175.9 0.2 fusion.26
  176.1 0.0 copy-done.11
  176.1 0.0 copy-start.6
  176.1 2.0 fusion.27
  178.1 0.0 copy-start.7
  178.1 0.0 all-gather.2.cloned.1.call-update
  178.1 0.3 fusion.12
  178.4 0.0 copy-done.5
  178.4 0.3 fusion.14
  178.8 573.8 %all-gather.2.cloned.1.call-done = bf16[256,2048]{1,0:T(8,128)(2,1)} async-done(((bf16[256,512]{1,0:T(8,128)(2,1)}), bf16[256,2048]{1,0:T(8,128)(2,1)}) %all-gather.2.cloned.1.call-update) | async-done | bytes 1048592 | tf_op jit(solution)/shard_map/all_gather | solution.py:81
  752.6 1.5 fusion.18
  754.1 0.0 copy-done.6
  754.1 1.5 fusion.20
  755.6 1.5 pad_maximum_fusion
  757.1 1.5 collective-permute-start.1
  758.6 0.0 copy-done.7
  758.6 0.6 collective-permute-start.6
  759.3 45.9 %collective-permute-done.1 = bf16[512,2048]{1,0:T(8,128)(2,1)} collective-permute-done((bf16[512,2048]{1,0:T(8,128)(2,1)}, bf16[512,2048]{1,0:T(8,128)(2,1)}, u32[]{:S(2)}, u32[]{:S(2)}) %collective-permute-start.1) | collective-permute-done | bytes 2097184 | tf_op jit(solution)/shard_map/ppermute | solution.py:19
  805.2 0.0 collective-permute-done.3
  805.2 49.2 %fusion = f32[1024,6400]{1,0:T(8,128)} fusion(bf16[2048,3200]{0,1:T(8,128)(2,1)} %maximum_select_fusion.2, bf16[2048,3200]{0,1:T(8,128)(2,1)} %collective-permute-done.3, pred[]{:T(512)S(6)} %eq.39, bf16[512,2048]{1,0:T(8,128)(2,1)} %collective-permute-done.1, bf16[256,2048]{1,0:T(8,128)(2,1)S(1)} %fusion.20, bf16[256,2048]{1,0:T(8,128)(2,1)S(1)} %bitcast.22), kind=kOutput, calls=%fused_computation.1 | convolution fusion | flops 26974093312 | bytes 56623104 | tf_op jit(solution)/shard_map/dot_general | solution.py:101
  854.4 0.0 copy-start
  854.4 9.4 %slice_reduce_fusion = (f32[512]{0:T(512)S(1)}, f32[512]{0:T(512)S(1)}) fusion(f32[1024,6400]{1,0:T(8,128)} %fusion), kind=kLoop, calls=%fused_computation.13 | loop fusion | flops 6552576 | bytes 26218496 | tf_op jit(solution)/shard_map/reduce_max | solution.py:29
  863.8 1.5 collective-permute-start.4
  865.4 0.0 collective-permute-done.6
  865.4 5.0 copy-done
  870.4 0.0 copy-start.8
  870.4 0.0 copy-start.9
  870.4 0.0 copy-start.10
  870.4 6.9 exponential_reduce_fusion.1
  877.3 1.5 collective-permute-start.7
  878.8 0.0 copy-done.8
  878.9 0.0 copy-done.9
  878.9 0.0 copy-done.10
  878.9 0.8 convert_reduce_fusion
  879.6 0.6 collective-permute-start.5
  880.2 0.0 collective-permute-done.4
  880.2 0.8 collective-permute-done.7
  881.0 5.7 pmax.7
  886.7 0.0 collective-permute-done.5
  886.7 5.8 all-reduce.1
  892.5 1.2 fusion.47
  893.7 22.3 %all-reduce = (f32[]{:T(128)}, f32[]{:T(128)}, f32[]{:T(128)}, f32[]{:T(128)}) all-reduce(f32[]{:T(128)} %get-tuple-element.25, f32[]{:T(128)} %get-tuple-element.27, f32[]{:T(128)} %get-tuple-element.19, f32[]{:T(128)} %get-tuple-element.17), channel_id=1, replica_groups=mesh['seq'=8,'vocab'=4] {'seq'}, use_global_device_ids=true, to_apply=%region_14.15 | all-reduce | flops 4 | bytes 32 | tf_op jit(solution)/shard_map/psum | solution.py:119
  (13 shorter events, 0.1 us)
Async XLA Ops:
  7.2 745.4 %all-gather.2.cloned.1.call-start = ((), (), s32[]{:S(2)}) async-start(), calls=%async_computation | async-start | bytes 1310720 | tf_op jit(solution)/shard_map/all_gather | solution.py:81
  7.2 144.6 %collective-permute-start.2 = (bf16[2048,1600]{0,1:T(8,128)(2,1)}, bf16[2048,1600]{0,1:T(8,128)(2,1)}, u32[]{:S(2)}, u32[]{:S(2)}) collective-permute-start(bf16[2048,1600]{0,1:T(8,128)(2,1)} %param.18), channel_id=1, source_target_pairs={{0,8},{4,12},{8,0},{12,4},{16,24},{20,28},{24,16},{28,20},{1,9},{5... | collective-permute-start | bytes 19660808 | tf_op jit(solution)/shard_map/ppermute | solution.py:19
  10.3 159.9 %copy-start.1 = (bf16[2,128,2048]{2,1,0:T(8,128)(2,1)S(1)}, bf16[2,128,2048]{2,1,0:T(8,128)(2,1)}, u32[]{:S(2)}) copy-start(bf16[2,128,2048]{2,1,0:T(8,128)(2,1)} %param.12) | copy-start | bytes 3145732
  10.3 163.3 %copy-start.2 = (bf16[2,128,2048]{2,1,0:T(8,128)(2,1)S(1)}, bf16[2,128,2048]{2,1,0:T(8,128)(2,1)}, u32[]{:S(2)}) copy-start(bf16[2,128,2048]{2,1,0:T(8,128)(2,1)} %param.13) | copy-start | bytes 3145732
  10.3 163.6 %copy-start.3 = (f32[2048]{0:T(1024)S(1)}, f32[2048]{0:T(1024)}, u32[]{:S(2)}) copy-start(f32[2048]{0:T(1024)} %param.22) | copy-start | bytes 24580
  167.4 8.4 copy-start.4
  167.4 8.7 copy-start.11
  167.4 637.8 %collective-permute-start.3 = (bf16[2048,3200]{0,1:T(8,128)(2,1)}, bf16[2048,3200]{0,1:T(8,128)(2,1)}, u32[]{:S(2)}, u32[]{:S(2)}) collective-permute-start(bf16[2048,3200]{0,1:T(8,128)(2,1)} %maximum_select_fusion.2), channel_id=1, source_target_pairs={{0,16},{4,20},{8,24},{12,28},{16,0},{20,4},{24,8},{28,12},{1,17},{... | collective-permute-start | bytes 39321608 | tf_op jit(solution)/shard_map/ppermute | solution.py:19
  170.2 4.8 collective-permute-start
  175.9 2.6 copy-start.5
  176.1 578.0 %copy-start.6 = (f32[2048]{0:T(1024)S(1)}, f32[2048]{0:T(1024)}, u32[]{:S(2)}) copy-start(f32[2048]{0:T(1024)} %param.23) | copy-start | bytes 24580
  178.1 580.5 %copy-start.7 = (s32[2,128]{1,0:T(2,128)S(1)}, s32[2,128]{1,0:T(2,128)}, u32[]{:S(2)}) copy-start(s32[2,128]{1,0:T(2,128)} %param.14) | copy-start | bytes 3076
  757.1 48.1 %collective-permute-start.1 = (bf16[512,2048]{1,0:T(8,128)(2,1)}, bf16[512,2048]{1,0:T(8,128)(2,1)}, u32[]{:S(2)}, u32[]{:S(2)}) collective-permute-start(bf16[512,2048]{1,0:T(8,128)(2,1)} %pad_maximum_fusion), channel_id=1, source_target_pairs={{0,4},{4,0},{8,12},{12,8},{16,20},{20,16},{24,28},{28,24},{1,5},{5... | collective-permute-start | bytes 6291464 | tf_op jit(solution)/shard_map/ppermute | solution.py:19
  758.6 106.7 %collective-permute-start.6 = (s32[512]{0:T(512)S(1)}, s32[512]{0:T(512)S(1)}, u32[]{:S(2)}, u32[]{:S(2)}) collective-permute-start(s32[512]{0:T(512)S(1)} %pad_add_fusion), channel_id=1, source_target_pairs={{0,4},{4,0},{8,12},{12,8},{16,20},{20,16},{24,28},{28,24},{1,5},{5... | collective-permute-start | bytes 6152 | tf_op jit(solution)/shard_map/ppermute | solution.py:19
  854.4 16.0 %copy-start = (f32[1024,6400]{1,0:T(8,128)S(1)}, f32[1024,6400]{1,0:T(8,128)}, u32[]{:S(2)}) copy-start(f32[1024,6400]{1,0:T(8,128)} %fusion) | copy-start | bytes 78643200
  863.8 16.3 %collective-permute-start.4 = (f32[512]{0:T(512)S(1)}, f32[512]{0:T(512)S(1)}, u32[]{:S(2)}, u32[]{:S(2)}) collective-permute-start(f32[512]{0:T(512)S(1)} %get-tuple-element.9), channel_id=1, source_target_pairs={{0,4},{4,0},{8,12},{12,8},{16,20},{20,16},{24,28},{28,24},{1,5},{5... | collective-permute-start | bytes 6152 | tf_op jit(solution)/shard_map/ppermute | solution.py:19
  870.4 8.4 copy-start.8
  870.4 8.4 copy-start.9
  870.4 8.4 copy-start.10
  877.3 3.6 collective-permute-start.7
  879.6 7.1 collective-permute-start.5
Sparse Core Ops, SparseCore 0:
  178.3 574.2 all-gather.1
where the time goes:
time: 927 us; the launch traced here: 926 us
  waiting for transfers between devices  763 us (82%)
  matrix products  51.1 us (6%)
  other arithmetic  40.7 us (4%)
  blocking collectives  33.8 us (4%)
  between operations  17.9 us (2%)
  starting transfers between devices  15.1 us (2%)
    all_gather x1, waiting for transfers between devices, shards(): mixed = lax.all_gather(partial_value, 'vocab', axis=1, tiled=True)  574 us
    ppermute x7, waiting for transfers between devices, partner_2(): return lax.ppermute(value, axis, pairs)  188 us
    dot_general x1, matrix products, shards(): jnp.dot(jnp.concatenate([all_rows, partner], axis=0), held_cols, preferre...  49.2 us
    psum x1, blocking collectives, shards(): summed = lax.psum((main_sum, mtp_sum), 'seq')  22.3 us
  transfers between devices with their start and end apart: 9, of which 5 were waited for; matrix products, arithmetic and copies ran while one was open for 8% of the time, Pallas kernels for 0%

commit v1 on v0

v1 whole, which is shorter than its diff:
```python
import functools

import jax
import jax.numpy as jnp
from jax import lax
from jax.experimental import pallas as pl
from jax.experimental.pallas import tpu as pltpu
from jax.sharding import PartitionSpec as P

EPSILON = 1e-06
MTP_WEIGHT = 0.3
CHUNK = 640


def from_behind(block, axis, distance):
    devices = range(lax.axis_size(axis))
    route = [(i - distance, i) for i in devices if i - distance in devices]
    return lax.ppermute(block, axis, route)


def normalize(values, gain_vec):
    values = values.astype(jnp.float32)
    mean_square = jnp.mean(values * values, axis=-1, keepdims=True)
    return values * lax.rsqrt(mean_square + EPSILON) * gain_vec


def join_stats(earlier, latter):
    highest = jnp.maximum(earlier[0], latter[0])
    exp_total = earlier[1] * jnp.exp(earlier[0] - highest) + latter[1] * jnp.exp(
        latter[0] - highest
    )
    return (highest, exp_total, earlier[2] + latter[2])


def seq_perm(value, bit):
    pairs = [(i, i ^ (1 << bit)) for i in range(lax.axis_size("seq"))]
    return lax.ppermute(value, "seq", pairs)


def vocab_perm(value, bit):
    pairs = [(i, i ^ (1 << bit)) for i in range(lax.axis_size("vocab"))]
    return lax.ppermute(value, "vocab", pairs)


def bits_of(axis):
    return list(reversed(range(lax.axis_size(axis).bit_length() - 1)))


def gather_pieces(own):
    pieces = [own]
    for bit in bits_of("seq"):
        held = pieces[0] if len(pieces) == 1 else jnp.concatenate(pieces, axis=0)
        pieces.append(seq_perm(held, bit))
    return pieces


def head_kernel(masks, at_ref, *refs):
    blocks = refs[: len(masks)]
    gain_ref, local_ref, w_ref, out_ref, rows_ref = refs[len(masks) :]
    rows, width = rows_ref.shape
    part = blocks[0].shape[2]
    values = [block[0].astype(jnp.float32) for block in blocks]
    square = sum(jnp.sum(v * v, axis=1, keepdims=True) for v in values)
    scale = lax.rsqrt(square / width + EPSILON)
    for mask, value in zip(masks, values):
        place = pl.ds(pl.multiple_of((at_ref[0] ^ mask) * part, part), part)
        rows_ref[:, place] = (value * scale * gain_ref[:, place]).astype(jnp.bfloat16)
    wanted = local_ref[0]
    cols = w_ref.shape[1]
    stats = None
    for start in range(0, cols, CHUNK):
        stop = min(start + CHUNK, cols)
        logits = jnp.dot(
            rows_ref[...], w_ref[:, start:stop], preferred_element_type=jnp.float32
        )
        ids = lax.broadcasted_iota(jnp.int32, logits.shape, 1) + start
        highest = jnp.max(logits, axis=1, keepdims=True)
        total = jnp.sum(jnp.exp(logits - highest), axis=1, keepdims=True)
        picked = jnp.sum(jnp.where(ids == wanted, logits, 0.0), axis=1, keepdims=True)
        fresh = (highest, total, picked)
        stats = fresh if stats is None else join_stats(stats, fresh)
    lane = lax.broadcasted_iota(jnp.int32, (rows, 128), 1)
    packed = jnp.where(lane == 0, stats[0], jnp.where(lane == 1, stats[1], stats[2]))
    out_ref[0] = packed.T[:8]


def head_stats(masks, at, blocks, gain, local, head_weight):
    count, rows, part = blocks[0].shape
    width, cols = head_weight.shape
    flops = 2 * count * rows * width * cols
    return pl.pallas_call(
        functools.partial(head_kernel, masks),
        out_shape=jax.ShapeDtypeStruct((count, 8, rows), jnp.float32),
        grid_spec=pltpu.PrefetchScalarGridSpec(
            num_scalar_prefetch=1,
            grid=(count,),
            in_specs=[pl.BlockSpec((1, rows, part), lambda i, at: (i, 0, 0)) for _ in blocks]
            + [
                pl.BlockSpec((1, width), lambda i, at: (0, 0)),
                pl.BlockSpec((1, rows, 1), lambda i, at: (i, 0, 0)),
                pl.BlockSpec((width, cols), lambda i, at: (0, 0)),
            ],
            out_specs=pl.BlockSpec((1, 8, rows), lambda i, at: (i, 0, 0)),
            scratch_shapes=[pltpu.VMEM((rows, width), jnp.bfloat16)],
        ),
        compiler_params=pltpu.CompilerParams(vmem_limit_bytes=48 * 2**20),
        cost_estimate=pl.CostEstimate(
            flops=flops, bytes_accessed=2 * (width * cols + count * rows * width), transcendentals=count * rows * cols
        ),
    )(at, *blocks, gain.reshape(1, -1), local, head_weight)


def join_packed(a, b):
    joined = join_stats((a[:, 0], a[:, 1], a[:, 2]), (b[:, 0], b[:, 1], b[:, 2]))
    return jnp.stack(joined, axis=1)


def finish(packed):
    held = packed[:, :3]
    for bit in reversed(bits_of("seq")):
        half = held.shape[0] // 2
        held = join_packed(held[:half], seq_perm(held[half:], bit))
    for bit in bits_of("vocab"):
        held = join_packed(held, vocab_perm(held, bit))
    return held[0, 0] + jnp.log(held[0, 1]) - held[0, 2]


def shards(
    hidden,
    embedded,
    targets,
    main_mask,
    mtp_mask,
    lengths,
    head_weight,
    projection,
    main_gain,
    hidden_gain,
    embed_gain,
    mtp_gain,
):
    batches, seq_len, model_width = hidden.shape
    rows = batches * seq_len
    seq_index = lax.axis_index("seq")
    vocab_index = lax.axis_index("vocab")
    vocab_count = lax.axis_size("vocab")
    cols = head_weight.shape[1]

    incoming = from_behind(hidden[:, seq_len - 1 :, :], "seq", 1)

    core = vocab_index & 1
    half = model_width // 2
    flat = hidden.reshape(1, rows, model_width)
    mine = lax.dynamic_slice_in_dim(flat, core * half, half, axis=2)
    other = lax.dynamic_slice_in_dim(flat, (1 - core) * half, half, axis=2)
    main_pieces = gather_pieces(mine)
    main_other = [other] + [vocab_perm(piece, 0) for piece in main_pieces[1:]]
    main_blocks = [jnp.concatenate(p, axis=0) for p in (main_pieces, main_other)]

    wanted = jnp.concatenate(gather_pieces(targets.reshape(1, rows)), axis=0)
    local = (wanted - (seq_index * vocab_count + vocab_index) * cols)[:, :, None]

    previous = jnp.concatenate([incoming, hidden[:, : seq_len - 1, :]], axis=1)
    joined = jnp.concatenate(
        [normalize(previous, hidden_gain), normalize(embedded, embed_gain)], axis=2
    )
    joined = joined.astype(jnp.bfloat16).reshape(rows, 2 * model_width)
    mixed = jnp.dot(joined, projection, preferred_element_type=jnp.float32).astype(jnp.bfloat16)
    masks = [0]
    held = [gather_pieces(mixed[None])]
    for bit in bits_of("vocab"):
        masks = masks + [mask | (1 << bit) for mask in masks]
        held = held + [[vocab_perm(piece, bit) for piece in pieces] for pieces in held]
    mtp_blocks = [jnp.concatenate(pieces, axis=0) for pieces in held]

    main_stats = head_stats((0, 1), core[None], main_blocks, main_gain, local, head_weight)
    mtp_stats = head_stats(tuple(masks), vocab_index[None], mtp_blocks, mtp_gain, local, head_weight)

    positions = seq_index * seq_len + lax.broadcasted_iota(jnp.int32, (batches, seq_len), 1)
    inside = positions + 1 < lengths[:, None]
    keep_main = ((main_mask == 1) & inside).astype(jnp.float32)
    keep_mtp = ((mtp_mask == 1) & (positions >= 1) & inside).astype(jnp.float32)
    main_tokens = keep_main * finish(main_stats).reshape(batches, seq_len)
    mtp_tokens = keep_mtp * finish(mtp_stats).reshape(batches, seq_len)
    sums = jnp.stack(
        [jnp.sum(main_tokens), jnp.sum(mtp_tokens), jnp.sum(keep_main), jnp.sum(keep_mtp)]
    )
    for bit in bits_of("seq"):
        sums = sums + seq_perm(sums, bit)
    total_loss = sums[0] / jnp.maximum(sums[2], 1.0) + MTP_WEIGHT * sums[1] / jnp.maximum(
        sums[3], 1.0
    )
    return (main_tokens, mtp_tokens, total_loss)


def solution(mesh):
    return jax.shard_map(
        shards,
        mesh=mesh,
        in_specs=(
            P(None, "seq", None),
            P(None, "seq", None),
            P(None, "seq"),
            P(None, "seq"),
            P(None, "seq"),
            P(),
            P(None, ("seq", "vocab")),
            P(None, "vocab"),
            P(),
            P(),
            P(),
            P(),
        ),
        out_specs=(P(None, "seq"), P(None, "seq"), P()),
        check_vma=False,
    )
```

time: 927 us -> 281 us (0.30)
  waiting for transfers between devices: 763 us -> 131 us
  Pallas kernels: 0 us -> 55.4 us
  matrix products: 51.1 us -> 1.24 us
  blocking collectives: 33.8 us -> 0 us
  starting transfers between devices: 15.1 us -> 39.7 us
  between operations: 17.9 us -> 4.78 us
  local copies, waits for them, and re-layouts: 5.1 us -> 15.4 us
    all_gather x1 -> x0, waiting for transfers between devices: 574 us -> none  [shards(): mixed = lax.all_gather(partial_value, 'vocab', axis=1, tiled=True)]
    ppermute x7 -> x37, waiting for transfers between devices: 188 us -> 131 us  [the longest x18 123 us: seq_perm(): return lax.ppermute(value, 'seq', pairs)]
    pallas_call x0 -> x2, Pallas kernels: none -> 55.4 us  [head_stats(): pl.pallas_call(functools.partial(head_kernel, masks), out_shape=jax.Shape...]
    dot_general x1 -> x0, matrix products: 49.2 us -> none  [shards(): jnp.dot(jnp.concatenate([all_rows, partner], axis=0), held_cols, preferre...]
    psum x2 -> x0, blocking collectives: 28 us -> none  [the longest x1 22.3 us: shards(): summed = lax.psum((main_sum, mtp_sum), 'seq')]
    ppermute x7 -> x37, starting transfers between devices: 11.6 us -> 34.8 us  [the longest x18 24.9 us: seq_perm(): return lax.ppermute(value, 'seq', pairs)]
    select_n x1 -> x0, other arithmetic: 15.6 us -> none  [shards(): jnp.where(upper_half, jnp.concatenate([received, held_cols], axis=1), jnp...]
    concatenate x2 -> x12, other arithmetic: 1.5 us -> 15.7 us  [the longest x4 8.88 us: shards(): mtp_blocks = [jnp.concatenate(pieces, axis=0) for pieces in held]]
  transfers between devices with their start and end apart: 9 -> 38, of which waited for: 5 -> 20; matrix products, arithmetic and copies ran while one was open for 8% -> 12% of each run, Pallas kernels for 0% -> 20%
where the time goes in v1:
time: 281 us; the launch traced here: 280 us
  waiting for transfers between devices  131 us (47%)
  Pallas kernels  55.4 us (20%)
  starting transfers between devices  39.7 us (14%)
  other arithmetic  32.5 us (12%)
  local copies, waits for them, and re-layouts  15.4 us (5%)
  between operations  4.78 us (2%)
    ppermute x18, waiting for transfers between devices, seq_perm(): return lax.ppermute(value, 'seq', pairs)  123 us
    pallas_call x2, Pallas kernels, head_stats(): pl.pallas_call(functools.partial(head_kernel, masks), out_shape=jax.Shape...  55.4 us
    ppermute x18, starting transfers between devices, seq_perm(): return lax.ppermute(value, 'seq', pairs)  24.9 us
    unnamed x37, local copies, waits for them, and re-layouts  11.7 us
    ppermute x19, starting transfers between devices, vocab_perm(): return lax.ppermute(value, 'vocab', pairs)  9.9 us
    concatenate x4, other arithmetic, shards(): mtp_blocks = [jnp.concatenate(pieces, axis=0) for pieces in held]  8.88 us
    ppermute x19, waiting for transfers between devices, vocab_perm(): return lax.ppermute(value, 'vocab', pairs)  8.59 us
  transfers between devices with their start and end apart: 38, of which 20 were waited for; matrix products, arithmetic and copies ran while one was open for 12% of the time, Pallas kernels for 20%

profile of v1, /device:TPU:0, one launch (start us, length us, event | category | flops | bytes accessed | tf_op | source)
XLA Modules:
  0.0 280.3 jit_solution(898976630895873348)
XLA Ops:
  0.6 0.9 slice.249
  1.6 4.9 %collective-permute-start.14 = (bf16[2,1,2048]{2,1,0:T(2,128)(2,1)S(1)}, bf16[2,1,2048]{2,1,0:T(2,128)(2,1)S(1)}, u32[]{:S(2)}, u32[]{:S(2)}) collective-permute-start(bf16[2,1,2048]{2,1,0:T(2,128)(2,1)S(1)} %slice.249), channel_id=1, source_target_pairs={{0,4},{4,8},{8,12},{12,16},{16,20},{20,24},{24,28},{1,5},{5,9},{9,... | collective-permute-start | bytes 24584 | tf_op jit(solution)/shard_map/ppermute | solution.py:18
  6.5 1.5 fusion
  8.0 1.5 fusion.2
  10.6 1.6 copy-done.17
  12.2 1.2 fusion.12
  13.5 2.7 collective-permute-start.15
  16.2 0.9 constant_dynamic-slice_fusion
  17.3 22.8 %collective-permute-done.15 = bf16[1,256,512]{2,1,0:T(8,128)(2,1)S(1)} collective-permute-done((bf16[1,256,512]{2,1,0:T(8,128)(2,1)S(1)}, bf16[1,256,512]{2,1,0:T(8,128)(2,1)S(1)}, u32[]{:S(2)}, u32[]{:S(2)}) %collective-permute-start.15) | collective-permute-done | bytes 262176 | tf_op jit(solution)/shard_map/ppermute | solution.py:37
  40.3 10.1 %collective-permute-done = bf16[1,256,1024]{2,1,0:T(8,128)(2,1)S(1)} collective-permute-done((bf16[1,256,1024]{2,1,0:T(8,128)(2,1)S(1)}, bf16[1,256,1024]{2,1,0:T(8,128)(2,1)S(1)}, u32[]{:S(2)}, u32[]{:S(2)}) %collective-permute-start) | collective-permute-done | bytes 524320 | tf_op jit(solution)/shard_map/ppermute | solution.py:37
  50.5 0.7 collective-permute-start.1
  51.2 10.5 %collective-permute-done.16 = bf16[2,256,512]{2,1,0:T(8,128)(2,1)} collective-permute-done((bf16[2,256,512]{2,1,0:T(8,128)(2,1)S(1)}, bf16[2,256,512]{2,1,0:T(8,128)(2,1)}, u32[]{:S(2)}, u32[]{:S(2)}) %collective-permute-start.16) | collective-permute-done | bytes 524320 | tf_op jit(solution)/shard_map/ppermute | solution.py:37
  61.7 1.1 pad_maximum_fusion.8
  62.9 1.6 collective-permute-start.17
  64.5 19.5 %collective-permute-done.1 = bf16[2,256,1024]{2,1,0:T(8,128)(2,1)S(1)} collective-permute-done((bf16[2,256,1024]{2,1,0:T(8,128)(2,1)S(1)}, bf16[2,256,1024]{2,1,0:T(8,128)(2,1)S(1)}, u32[]{:S(2)}, u32[]{:S(2)}) %collective-permute-start.1) | collective-permute-done | bytes 1048608 | tf_op jit(solution)/shard_map/ppermute | solution.py:37
  84.0 1.5 pad_maximum_fusion.2
  85.5 1.6 collective-permute-start.2
  87.1 1.0 collective-permute-done.17
  88.0 1.5 collective-permute-start.21
  89.6 1.5 collective-permute-start.6
  91.5 2.5 collective-permute-done.6
  94.0 1.1 collective-permute-start.7
  95.2 2.5 collective-permute-done.7
  97.6 1.6 collective-permute-start.8
  99.3 34.3 %collective-permute-done.8 = s32[4,256]{1,0:T(4,128)S(1)} collective-permute-done((s32[4,256]{1,0:T(4,128)S(1)}, s32[4,256]{1,0:T(4,128)S(1)}, u32[]{:S(2)}, u32[]{:S(2)}) %collective-permute-start.8) | collective-permute-done | bytes 4128 | tf_op jit(solution)/shard_map/ppermute | solution.py:37
  133.5 1.6 collective-permute-start.19
  135.3 7.0 %collective-permute-done.19 = bf16[1,256,512]{2,1,0:T(8,128)(2,1)S(1)} collective-permute-done((bf16[1,256,512]{2,1,0:T(8,128)(2,1)S(1)}, bf16[1,256,512]{2,1,0:T(8,128)(2,1)S(1)}, u32[]{:S(2)}, u32[]{:S(2)}) %collective-permute-start.19) | collective-permute-done | bytes 262176 | tf_op jit(solution)/shard_map/ppermute | solution.py:42
  142.3 1.5 collective-permute-start.20
  144.6 9.8 %copy.38.refs_4_.refs_6_ = bf16[2048,1600]{1,0:T(8,128)(2,1)} copy(bf16[2048,1600]{0,1:T(8,128)(2,1)} %param.18) | data formatting | bytes 13107200 | tf_op args[6]
  154.4 0.8 copy.35
  155.6 1.0 add_subtract_fusion.refs_3_.refs_5_
  157.2 1.6 pad_maximum_fusion.3.refs_0_
  159.4 1.6 pad_maximum_fusion.4.refs_1_
  161.0 3.0 %pad_maximum_fusion.5.refs_2_ = bf16[8,256,512]{2,1,0:T(8,128)(2,1)} fusion(bf16[4,256,512]{2,1,0:T(8,128)(2,1)} %collective-permute-done.25, bf16[2,256,512]{2,1,0:T(8,128)(2,1)} %collective-permute-done.24, bf16[1,256,512]{2,1,0:T(8,128)(2,1)S(1)} %copy-done.11, bf16[1,256,512]{2,1,0:T(8,128)(2,1)S(1)} %copy-done.9), kind=kLoop, calls=%fused_computation.14 | loop fusion | flops 3145728 | bytes 4194304 | tf_op jit(solution)/shard_map/concatenate | solution.py:174
  164.1 2.7 pad_maximum_fusion.6.refs_3_
  166.8 27.7 %shard_map.140 = f32[8,8,256]{2,1,0:T(8,128)S(1)} custom-call(s32[1]{0:T(128)} %bitcast.17.at_ref, bf16[8,256,512]{2,1,0:T(8,128)(2,1)S(1)} %pad_maximum_fusion.3.refs_0_, bf16[8,256,512]{2,1,0:T(8,128)(2,1)S(1)} %pad_maximum_fusion.4.refs_1_, bf16[8,256,512]{2,1,0:T(8,128)(2,1)} %pad_maximum_fusion.5.refs_2_, ...), custom_call_target="tpu_custom_call" | custom-call | flops 13421772800 | bytes 14942208 | tf_op jit(solution)/shard_map/pallas_call | solution.py:91
  194.5 1.6 collective-permute-start.30
  196.2 2.2 collective-permute-done.30
  199.1 3.0 %collective-permute-done.31 = f32[2,3,256]{2,1,0:T(4,128)S(1)} collective-permute-done((f32[2,3,256]{2,1,0:T(4,128)S(1)}, f32[2,3,256]{2,1,0:T(4,128)S(1)}, u32[]{:S(2)}, u32[]{:S(2)}) %collective-permute-start.31) | collective-permute-done | bytes 6176 | tf_op jit(solution)/shard_map/ppermute | solution.py:37
  202.2 2.1 collective-permute-start.32
  204.3 1.8 pad_maximum_fusion.refs_0_
  206.0 0.7 collective-permute-done.32
  206.8 0.8 collective-permute-start.33
  207.6 2.3 pad_maximum_fusion.1.refs_1_
  209.9 27.7 %shard_map.139 = f32[8,8,256]{2,1,0:T(8,128)S(1)} custom-call(s32[1]{0:T(128)} %bitcast.at_ref, bf16[8,256,1024]{2,1,0:T(8,128)(2,1)S(1)} %pad_maximum_fusion.refs_0_, bf16[8,256,1024]{2,1,0:T(8,128)(2,1)} %pad_maximum_fusion.1.refs_1_, f32[1,2048]{1,0:T(1,128)S(1)} %bitcast.47, s32[8,256,1]{2,1,0:T(8,128)S(1)} %add_subtract_fusion.refs_3_.refs_5_, ...), custom_call_target="tpu_custom_call" | custom-call | flops 13421772800 | bytes 14942208 | tf_op jit(solution)/shard_map/pallas_call | solution.py:91
  237.6 1.6 collective-permute-start.9
  239.2 2.2 collective-permute-done.9
  241.4 1.4 collective-permute-start.10
  242.9 2.2 collective-permute-done.10
  245.2 2.1 collective-permute-start.11
  247.3 2.5 collective-permute-done.11
  249.8 1.4 collective-permute-start.12
  251.2 1.3 fusion.35
  252.4 1.0 collective-permute-done.12
  254.7 1.2 fusion.34
  256.6 2.6 pad_maximum_fusion.22
  259.2 2.0 collective-permute-start.35
  261.2 2.4 collective-permute-done.35
  263.7 2.6 fusion.40
  266.3 1.3 collective-permute-start.36
  267.6 2.2 collective-permute-done.36
  269.8 2.6 fusion.41
  272.4 1.6 collective-permute-start.37
  274.0 2.0 collective-permute-done.37
  (109 shorter events, 8.3 us)
Async XLA Ops:
  0.6 8.9 %copy-start.2 = (bf16[2,128,2048]{2,1,0:T(8,128)(2,1)S(1)}, bf16[2,128,2048]{2,1,0:T(8,128)(2,1)}, u32[]{:S(2)}) copy-start(bf16[2,128,2048]{2,1,0:T(8,128)(2,1)} %param.12) | copy-start | bytes 3145732
  1.6 7.9 %collective-permute-start.14 = (bf16[2,1,2048]{2,1,0:T(2,128)(2,1)S(1)}, bf16[2,1,2048]{2,1,0:T(2,128)(2,1)S(1)}, u32[]{:S(2)}, u32[]{:S(2)}) collective-permute-start(bf16[2,1,2048]{2,1,0:T(2,128)(2,1)S(1)} %slice.249), channel_id=1, source_target_pairs={{0,4},{4,8},{8,12},{12,16},{16,20},{20,24},{24,28},{1,5},{5,9},{9,... | collective-permute-start | bytes 24584 | tf_op jit(solution)/shard_map/ppermute | solution.py:18
  9.6 0.8 copy-start.13
  10.0 2.2 copy-start.17
  13.5 26.7 %collective-permute-start.15 = (bf16[1,256,512]{2,1,0:T(8,128)(2,1)S(1)}, bf16[1,256,512]{2,1,0:T(8,128)(2,1)S(1)}, u32[]{:S(2)}, u32[]{:S(2)}) collective-permute-start(bf16[1,256,512]{2,1,0:T(8,128)(2,1)S(1)} %fusion.12), channel_id=1, source_target_pairs={{0,16},{4,20},{8,24},{12,28},{16,0},{20,4},{24,8},{28,12},{1,17},{... | collective-permute-start | bytes 786440 | tf_op jit(solution)/shard_map/ppermute | solution.py:37
  17.0 33.3 %collective-permute-start = (bf16[1,256,1024]{2,1,0:T(8,128)(2,1)S(1)}, bf16[1,256,1024]{2,1,0:T(8,128)(2,1)S(1)}, u32[]{:S(2)}, u32[]{:S(2)}) collective-permute-start(bf16[1,256,1024]{2,1,0:T(8,128)(2,1)S(1)} %get-tuple-element.22), channel_id=1, source_target_pairs={{0,16},{4,20},{8,24},{12,28},{16,0},{20,4},{24,8},{28,12},{1,17},{... | collective-permute-start | bytes 1572872 | tf_op jit(solution)/shard_map/ppermute | solution.py:37
  40.2 21.5 %collective-permute-start.16 = (bf16[2,256,512]{2,1,0:T(8,128)(2,1)S(1)}, bf16[2,256,512]{2,1,0:T(8,128)(2,1)}, u32[]{:S(2)}, u32[]{:S(2)}) collective-permute-start(bf16[2,256,512]{2,1,0:T(8,128)(2,1)S(1)} %pad_maximum_fusion.9), channel_id=1, source_target_pairs={{0,8},{4,12},{8,0},{12,4},{16,24},{20,28},{24,16},{28,20},{1,9},{5... | collective-permute-start | bytes 1572872 | tf_op jit(solution)/shard_map/ppermute | solution.py:37
  50.5 33.5 %collective-permute-start.1 = (bf16[2,256,1024]{2,1,0:T(8,128)(2,1)S(1)}, bf16[2,256,1024]{2,1,0:T(8,128)(2,1)S(1)}, u32[]{:S(2)}, u32[]{:S(2)}) collective-permute-start(bf16[2,256,1024]{2,1,0:T(8,128)(2,1)S(1)} %pad_maximum_fusion.7), channel_id=1, source_target_pairs={{0,8},{4,12},{8,0},{12,4},{16,24},{20,28},{24,16},{28,20},{1,9},{5... | collective-permute-start | bytes 3145736 | tf_op jit(solution)/shard_map/ppermute | solution.py:37
  62.9 26.7 %copy-start.12 = (s32[2,128]{1,0:T(2,128)S(1)}, s32[2,128]{1,0:T(2,128)}, u32[]{:S(2)}) copy-start(s32[2,128]{1,0:T(2,128)} %param.14) | copy-start | bytes 3076
  62.9 25.2 %collective-permute-start.17 = (bf16[4,256,512]{2,1,0:T(8,128)(2,1)S(1)}, bf16[4,256,512]{2,1,0:T(8,128)(2,1)}, u32[]{:S(2)}, u32[]{:S(2)}) collective-permute-start(bf16[4,256,512]{2,1,0:T(8,128)(2,1)S(1)} %pad_maximum_fusion.8), channel_id=1, source_target_pairs={{0,4},{4,0},{8,12},{12,8},{16,20},{20,16},{24,28},{28,24},{1,5},{5... | collective-permute-start | bytes 3145736 | tf_op jit(solution)/shard_map/ppermute | solution.py:37
  85.5 78.5 %collective-permute-start.2 = (bf16[4,256,1024]{2,1,0:T(8,128)(2,1)}, bf16[4,256,1024]{2,1,0:T(8,128)(2,1)}, u32[]{:S(2)}, u32[]{:S(2)}) collective-permute-start(bf16[4,256,1024]{2,1,0:T(8,128)(2,1)} %pad_maximum_fusion.2), channel_id=1, source_target_pairs={{0,4},{4,0},{8,12},{12,8},{16,20},{20,16},{24,28},{28,24},{1,5},{5... | collective-permute-start | bytes 6291464 | tf_op jit(solution)/shard_map/ppermute | solution.py:37
  88.0 55.7 %collective-permute-start.21 = (bf16[4,256,512]{2,1,0:T(8,128)(2,1)}, bf16[4,256,512]{2,1,0:T(8,128)(2,1)}, u32[]{:S(2)}, u32[]{:S(2)}) collective-permute-start(bf16[4,256,512]{2,1,0:T(8,128)(2,1)} %collective-permute-done.17), channel_id=1, source_target_pairs={{0,2},{1,3},{2,0},{3,1},{4,6},{5,7},{6,4},{7,5},{8,10},{9,11},{10,... | collective-permute-start | bytes 3145736 | tf_op jit(solution)/shard_map/ppermute | solution.py:42
  89.6 4.5 %collective-permute-start.6 = (s32[1,256]{1,0:T(1,128)S(1)}, s32[1,256]{1,0:T(1,128)S(1)}, u32[]{:S(2)}, u32[]{:S(2)}) collective-permute-start(s32[1,256]{1,0:T(1,128)S(1)} %bitcast.52), channel_id=1, source_target_pairs={{0,16},{4,20},{8,24},{12,28},{16,0},{20,4},{24,8},{28,12},{1,17},{... | collective-permute-start | bytes 3080 | tf_op jit(solution)/shard_map/ppermute | solution.py:37
  91.0 42.5 %collective-permute-start.18 = (bf16[1,256,512]{2,1,0:T(8,128)(2,1)S(1)}, bf16[1,256,512]{2,1,0:T(8,128)(2,1)S(1)}, u32[]{:S(2)}, u32[]{:S(2)}) collective-permute-start(bf16[1,256,512]{2,1,0:T(8,128)(2,1)S(1)} %fusion.12), channel_id=1, source_target_pairs={{0,2},{1,3},{2,0},{3,1},{4,6},{5,7},{6,4},{7,5},{8,10},{9,11},{10,... | collective-permute-start | bytes 786440 | tf_op jit(solution)/shard_map/ppermute | solution.py:42
  94.0 3.6 %collective-permute-start.7 = (s32[2,256]{1,0:T(2,128)S(1)}, s32[2,256]{1,0:T(2,128)S(1)}, u32[]{:S(2)}, u32[]{:S(2)}) collective-permute-start(s32[2,256]{1,0:T(2,128)S(1)} %pad_add_fusion.1), channel_id=1, source_target_pairs={{0,8},{4,12},{8,0},{12,4},{16,24},{20,28},{24,16},{28,20},{1,9},{5... | collective-permute-start | bytes 6152 | tf_op jit(solution)/shard_map/ppermute | solution.py:37
  97.6 35.9 %collective-permute-start.8 = (s32[4,256]{1,0:T(4,128)S(1)}, s32[4,256]{1,0:T(4,128)S(1)}, u32[]{:S(2)}, u32[]{:S(2)}) collective-permute-start(s32[4,256]{1,0:T(4,128)S(1)} %pad_add_fusion), channel_id=1, source_target_pairs={{0,4},{4,0},{8,12},{12,8},{16,20},{20,16},{24,28},{28,24},{1,5},{5... | collective-permute-start | bytes 12296 | tf_op jit(solution)/shard_map/ppermute | solution.py:37
  99.2 35.9 %collective-permute-start.22 = (bf16[1,256,512]{2,1,0:T(8,128)(2,1)S(1)}, bf16[1,256,512]{2,1,0:T(8,128)(2,1)S(1)}, u32[]{:S(2)}, u32[]{:S(2)}) collective-permute-start(bf16[1,256,512]{2,1,0:T(8,128)(2,1)S(1)} %fusion.12), channel_id=1, source_target_pairs={{0,1},{1,0},{2,3},{3,2},{4,5},{5,4},{6,7},{7,6},{8,9},{9,8},{10,11... | collective-permute-start | bytes 786440 | tf_op jit(solution)/shard_map/ppermute | solution.py:42
  133.5 25.4 %collective-permute-start.25 = (bf16[4,256,512]{2,1,0:T(8,128)(2,1)}, bf16[4,256,512]{2,1,0:T(8,128)(2,1)}, u32[]{:S(2)}, u32[]{:S(2)}) collective-permute-start(bf16[4,256,512]{2,1,0:T(8,128)(2,1)} %collective-permute-done.17), channel_id=1, source_target_pairs={{0,1},{1,0},{2,3},{3,2},{4,5},{5,4},{6,7},{7,6},{8,9},{9,8},{10,11... | collective-permute-start | bytes 3145736 | tf_op jit(solution)/shard_map/ppermute | solution.py:42
  133.5 10.8 %copy-start.4 = (bf16[1,256,512]{2,1,0:T(8,128)(2,1)}, bf16[1,256,512]{2,1,0:T(8,128)(2,1)S(1)}, u32[]{:S(2)}) copy-start(bf16[1,256,512]{2,1,0:T(8,128)(2,1)S(1)} %collective-permute-done.18) | copy-start | bytes 786436
  133.5 8.7 %collective-permute-start.19 = (bf16[1,256,512]{2,1,0:T(8,128)(2,1)S(1)}, bf16[1,256,512]{2,1,0:T(8,128)(2,1)S(1)}, u32[]{:S(2)}, u32[]{:S(2)}) collective-permute-start(bf16[1,256,512]{2,1,0:T(8,128)(2,1)S(1)} %collective-permute-done.15), channel_id=1, source_target_pairs={{0,2},{1,3},{2,0},{3,1},{4,6},{5,7},{6,4},{7,5},{8,10},{9,11},{10,... | collective-permute-start | bytes 786440 | tf_op jit(solution)/shard_map/ppermute | solution.py:42
  135.1 9.2 %copy-start.8 = (bf16[1,256,512]{2,1,0:T(8,128)(2,1)}, bf16[1,256,512]{2,1,0:T(8,128)(2,1)S(1)}, u32[]{:S(2)}) copy-start(bf16[1,256,512]{2,1,0:T(8,128)(2,1)S(1)} %collective-permute-done.22) | copy-start | bytes 786436
  135.1 8.7 %collective-permute-start.23 = (bf16[1,256,512]{2,1,0:T(8,128)(2,1)S(1)}, bf16[1,256,512]{2,1,0:T(8,128)(2,1)S(1)}, u32[]{:S(2)}, u32[]{:S(2)}) collective-permute-start(bf16[1,256,512]{2,1,0:T(8,128)(2,1)S(1)} %collective-permute-done.15), channel_id=1, source_target_pairs={{0,1},{1,0},{2,3},{3,2},{4,5},{5,4},{6,7},{7,6},{8,9},{9,8},{10,11... | collective-permute-start | bytes 786440 | tf_op jit(solution)/shard_map/ppermute | solution.py:42
  142.3 2.1 copy-start.6
  142.3 14.4 %collective-permute-start.20 = (bf16[2,256,512]{2,1,0:T(8,128)(2,1)}, bf16[2,256,512]{2,1,0:T(8,128)(2,1)}, u32[]{:S(2)}, u32[]{:S(2)}) collective-permute-start(bf16[2,256,512]{2,1,0:T(8,128)(2,1)} %collective-permute-done.16), channel_id=1, source_target_pairs={{0,2},{1,3},{2,0},{3,1},{4,6},{5,7},{6,4},{7,5},{8,10},{9,11},{10,... | collective-permute-start | bytes 1572872 | tf_op jit(solution)/shard_map/ppermute | solution.py:42
  143.8 20.3 %collective-permute-start.29 = (bf16[4,256,512]{2,1,0:T(8,128)(2,1)}, bf16[4,256,512]{2,1,0:T(8,128)(2,1)}, u32[]{:S(2)}, u32[]{:S(2)}) collective-permute-start(bf16[4,256,512]{2,1,0:T(8,128)(2,1)} %collective-permute-done.21), channel_id=1, source_target_pairs={{0,1},{1,0},{2,3},{3,2},{4,5},{5,4},{6,7},{7,6},{8,9},{9,8},{10,11... | collective-permute-start | bytes 3145736 | tf_op jit(solution)/shard_map/ppermute | solution.py:42
  143.8 0.7 copy-start.10
  143.8 15.0 %collective-permute-start.24 = (bf16[2,256,512]{2,1,0:T(8,128)(2,1)}, bf16[2,256,512]{2,1,0:T(8,128)(2,1)}, u32[]{:S(2)}, u32[]{:S(2)}) collective-permute-start(bf16[2,256,512]{2,1,0:T(8,128)(2,1)} %collective-permute-done.16), channel_id=1, source_target_pairs={{0,1},{1,0},{2,3},{3,2},{4,5},{5,4},{6,7},{7,6},{8,9},{9,8},{10,11... | collective-permute-start | bytes 1572872 | tf_op jit(solution)/shard_map/ppermute | solution.py:42
  156.6 2.2 copy-start.5
  156.6 2.3 copy-start.7
  156.6 7.5 %collective-permute-start.28 = (bf16[2,256,512]{2,1,0:T(8,128)(2,1)}, bf16[2,256,512]{2,1,0:T(8,128)(2,1)S(1)}, u32[]{:S(2)}, u32[]{:S(2)}) collective-permute-start(bf16[2,256,512]{2,1,0:T(8,128)(2,1)} %collective-permute-done.20), channel_id=1, source_target_pairs={{0,1},{1,0},{2,3},{3,2},{4,5},{5,4},{6,7},{7,6},{8,9},{9,8},{10,11... | collective-permute-start | bytes 1572872 | tf_op jit(solution)/shard_map/ppermute | solution.py:42
  158.8 2.2 copy-start.9
  158.8 2.2 copy-start.11
  158.8 5.3 %collective-permute-start.26 = (bf16[1,256,512]{2,1,0:T(8,128)(2,1)S(1)}, bf16[1,256,512]{2,1,0:T(8,128)(2,1)S(1)}, u32[]{:S(2)}, u32[]{:S(2)}) collective-permute-start(bf16[1,256,512]{2,1,0:T(8,128)(2,1)S(1)} %copy-done.5), channel_id=1, source_target_pairs={{0,1},{1,0},{2,3},{3,2},{4,5},{5,4},{6,7},{7,6},{8,9},{9,8},{10,11... | collective-permute-start | bytes 786440 | tf_op jit(solution)/shard_map/ppermute | solution.py:42
  158.9 5.2 %collective-permute-start.27 = (bf16[1,256,512]{2,1,0:T(8,128)(2,1)S(1)}, bf16[1,256,512]{2,1,0:T(8,128)(2,1)S(1)}, u32[]{:S(2)}, u32[]{:S(2)}) collective-permute-start(bf16[1,256,512]{2,1,0:T(8,128)(2,1)S(1)} %copy-done.7), channel_id=1, source_target_pairs={{0,1},{1,0},{2,3},{3,2},{4,5},{5,4},{6,7},{7,6},{8,9},{9,8},{10,11... | collective-permute-start | bytes 786440 | tf_op jit(solution)/shard_map/ppermute | solution.py:42
  164.0 2.9 %copy-start = (f32[2048]{0:T(1024)S(1)}, f32[2048]{0:T(1024)}, u32[]{:S(2)}) copy-start(f32[2048]{0:T(1024)} %param.23) | copy-start | bytes 24580
  164.0 43.6 %collective-permute-start.5 = (bf16[4,256,1024]{2,1,0:T(8,128)(2,1)}, bf16[4,256,1024]{2,1,0:T(8,128)(2,1)S(1)}, u32[]{:S(2)}, u32[]{:S(2)}) collective-permute-start(bf16[4,256,1024]{2,1,0:T(8,128)(2,1)} %collective-permute-done.2), channel_id=1, source_target_pairs={{0,1},{1,0},{2,3},{3,2},{4,5},{5,4},{6,7},{7,6},{8,9},{9,8},{10,11... | collective-permute-start | bytes 6291464 | tf_op jit(solution)/shard_map/ppermute | solution.py:42
  194.5 3.8 %collective-permute-start.30 = (f32[4,3,256]{2,1,0:T(4,128)S(1)}, f32[4,3,256]{2,1,0:T(4,128)S(1)}, u32[]{:S(2)}, u32[]{:S(2)}) collective-permute-start(f32[4,3,256]{2,1,0:T(4,128)S(1)} %slice.308), channel_id=1, source_target_pairs={{0,4},{4,0},{8,12},{12,8},{16,20},{20,16},{24,28},{28,24},{1,5},{5... | collective-permute-start | bytes 36872 | tf_op jit(solution)/shard_map/ppermute | solution.py:37
  198.4 3.7 %collective-permute-start.31 = (f32[2,3,256]{2,1,0:T(4,128)S(1)}, f32[2,3,256]{2,1,0:T(4,128)S(1)}, u32[]{:S(2)}, u32[]{:S(2)}) collective-permute-start(f32[2,3,256]{2,1,0:T(4,128)S(1)} %pad_maximum_fusion.10), channel_id=1, source_target_pairs={{0,8},{4,12},{8,0},{12,4},{16,24},{20,28},{24,16},{28,20},{1,9},{5... | collective-permute-start | bytes 18440 | tf_op jit(solution)/shard_map/ppermute | solution.py:37
  198.5 9.1 %collective-permute-start.3 = (bf16[1,256,1024]{2,1,0:T(8,128)(2,1)S(1)}, bf16[1,256,1024]{2,1,0:T(8,128)(2,1)S(1)}, u32[]{:S(2)}, u32[]{:S(2)}) collective-permute-start(bf16[1,256,1024]{2,1,0:T(8,128)(2,1)S(1)} %collective-permute-done), channel_id=1, source_target_pairs={{0,1},{1,0},{2,3},{3,2},{4,5},{5,4},{6,7},{7,6},{8,9},{9,8},{10,11... | collective-permute-start | bytes 1572872 | tf_op jit(solution)/shard_map/ppermute | solution.py:42
  198.6 9.0 %collective-permute-start.4 = (bf16[2,256,1024]{2,1,0:T(8,128)(2,1)S(1)}, bf16[2,256,1024]{2,1,0:T(8,128)(2,1)S(1)}, u32[]{:S(2)}, u32[]{:S(2)}) collective-permute-start(bf16[2,256,1024]{2,1,0:T(8,128)(2,1)S(1)} %collective-permute-done.1), channel_id=1, source_target_pairs={{0,1},{1,0},{2,3},{3,2},{4,5},{5,4},{6,7},{7,6},{8,9},{9,8},{10,11... | collective-permute-start | bytes 3145736 | tf_op jit(solution)/shard_map/ppermute | solution.py:42
  202.2 5.4 %copy-start.3 = (bf16[1,256,1024]{2,1,0:T(8,128)(2,1)S(1)}, bf16[1,256,1024]{2,1,0:T(8,128)(2,1)}, u32[]{:S(2)}) copy-start(bf16[1,256,1024]{2,1,0:T(8,128)(2,1)} %get-tuple-element.21) | copy-start | bytes 1572868
  202.2 4.6 %collective-permute-start.32 = (f32[1,3,256]{2,1,0:T(4,128)S(1)}, f32[1,3,256]{2,1,0:T(4,128)S(1)}, u32[]{:S(2)}, u32[]{:S(2)}) collective-permute-start(f32[1,3,256]{2,1,0:T(4,128)S(1)} %pad_maximum_fusion.14), channel_id=1, source_target_pairs={{0,16},{4,20},{8,24},{12,28},{16,0},{20,4},{24,8},{28,12},{1,17},{... | collective-permute-start | bytes 9224 | tf_op jit(solution)/shard_map/ppermute | solution.py:37
  206.8 32.4 %collective-permute-start.33 = (f32[1,3,256]{2,1,0:T(4,128)S(1)}, f32[1,3,256]{2,1,0:T(4,128)S(1)}, u32[]{:S(2)}, u32[]{:S(2)}) collective-permute-start(f32[1,3,256]{2,1,0:T(4,128)S(1)} %pad_maximum_fusion.20), channel_id=1, source_target_pairs={{0,2},{1,3},{2,0},{3,1},{4,6},{5,7},{6,4},{7,5},{8,10},{9,11},{10,... | collective-permute-start | bytes 9224 | tf_op jit(solution)/shard_map/ppermute | solution.py:42
  207.6 2.3 copy-start.1
  209.9 41.3 %copy-start.14 = (s32[2]{0:T(128)S(1)}, s32[2]{0:T(128)}, u32[]{:S(2)}) copy-start(s32[2]{0:T(128)} %param.17) | copy-start | bytes 28
  209.9 41.3 %copy-start.15 = (s32[2,128]{1,0:T(2,128)S(1)}, s32[2,128]{1,0:T(2,128)}, u32[]{:S(2)}) copy-start(s32[2,128]{1,0:T(2,128)} %param.16) | copy-start | bytes 3076
  209.9 44.8 %copy-start.16 = (s32[2,128]{1,0:T(2,128)S(1)}, s32[2,128]{1,0:T(2,128)}, u32[]{:S(2)}) copy-start(s32[2,128]{1,0:T(2,128)} %param.15) | copy-start | bytes 3076
  237.6 3.8 %collective-permute-start.9 = (f32[4,3,256]{2,1,0:T(4,128)S(1)}, f32[4,3,256]{2,1,0:T(4,128)S(1)}, u32[]{:S(2)}, u32[]{:S(2)}) collective-permute-start(f32[4,3,256]{2,1,0:T(4,128)S(1)} %slice.283), channel_id=1, source_target_pairs={{0,4},{4,0},{8,12},{12,8},{16,20},{20,16},{24,28},{28,24},{1,5},{5... | collective-permute-start | bytes 36872 | tf_op jit(solution)/shard_map/ppermute | solution.py:37
  241.4 3.7 %collective-permute-start.10 = (f32[2,3,256]{2,1,0:T(4,128)S(1)}, f32[2,3,256]{2,1,0:T(4,128)S(1)}, u32[]{:S(2)}, u32[]{:S(2)}) collective-permute-start(f32[2,3,256]{2,1,0:T(4,128)S(1)} %pad_maximum_fusion.12), channel_id=1, source_target_pairs={{0,8},{4,12},{8,0},{12,4},{16,24},{20,28},{24,16},{28,20},{1,9},{5... | collective-permute-start | bytes 18440 | tf_op jit(solution)/shard_map/ppermute | solution.py:37
  242.8 4.4 %collective-permute-start.34 = (f32[1,3,256]{2,1,0:T(4,128)S(1)}, f32[1,3,256]{2,1,0:T(4,128)S(1)}, u32[]{:S(2)}, u32[]{:S(2)}) collective-permute-start(f32[1,3,256]{2,1,0:T(4,128)S(1)} %pad_maximum_fusion.21), channel_id=1, source_target_pairs={{0,1},{1,0},{2,3},{3,2},{4,5},{5,4},{6,7},{7,6},{8,9},{9,8},{10,11... | collective-permute-start | bytes 9224 | tf_op jit(solution)/shard_map/ppermute | solution.py:42
  245.2 4.6 %collective-permute-start.11 = (f32[1,3,256]{2,1,0:T(4,128)S(1)}, f32[1,3,256]{2,1,0:T(4,128)S(1)}, u32[]{:S(2)}, u32[]{:S(2)}) collective-permute-start(f32[1,3,256]{2,1,0:T(4,128)S(1)} %pad_maximum_fusion.16), channel_id=1, source_target_pairs={{0,16},{4,20},{8,24},{12,28},{16,0},{20,4},{24,8},{28,12},{1,17},{... | collective-permute-start | bytes 9224 | tf_op jit(solution)/shard_map/ppermute | solution.py:37
  249.8 3.7 %collective-permute-start.12 = (f32[1,3,256]{2,1,0:T(4,128)S(1)}, f32[1,3,256]{2,1,0:T(4,128)S(1)}, u32[]{:S(2)}, u32[]{:S(2)}) collective-permute-start(f32[1,3,256]{2,1,0:T(4,128)S(1)} %pad_maximum_fusion.18), channel_id=1, source_target_pairs={{0,2},{1,3},{2,0},{3,1},{4,6},{5,7},{6,4},{7,5},{8,10},{9,11},{10,... | collective-permute-start | bytes 9224 | tf_op jit(solution)/shard_map/ppermute | solution.py:42
  253.5 1.2 collective-permute-start.13
  259.2 4.5 %collective-permute-start.35 = (f32[4]{0:T(128)S(1)}, f32[4]{0:T(128)S(1)}, u32[]{:S(2)}, u32[]{:S(2)}) collective-permute-start(f32[4]{0:T(128)S(1)} %pad_maximum_fusion.22), channel_id=1, source_target_pairs={{0,16},{4,20},{8,24},{12,28},{16,0},{20,4},{24,8},{28,12},{1,17},{... | collective-permute-start | bytes 56 | tf_op jit(solution)/shard_map/ppermute | solution.py:37
  266.3 3.6 %collective-permute-start.36 = (f32[4]{0:T(128)S(1)}, f32[4]{0:T(128)S(1)}, u32[]{:S(2)}, u32[]{:S(2)}) collective-permute-start(f32[4]{0:T(128)S(1)} %fusion.40), channel_id=1, source_target_pairs={{0,8},{4,12},{8,0},{12,4},{16,24},{20,28},{24,16},{28,20},{1,9},{5... | collective-permute-start | bytes 56 | tf_op jit(solution)/shard_map/ppermute | solution.py:37
  272.4 3.6 %collective-permute-start.37 = (f32[4]{0:T(128)S(1)}, f32[4]{0:T(128)S(1)}, u32[]{:S(2)}, u32[]{:S(2)}) collective-permute-start(f32[4]{0:T(128)S(1)} %fusion.41), channel_id=1, source_target_pairs={{0,4},{4,0},{8,12},{12,8},{16,20},{20,16},{24,28},{28,24},{1,5},{5... | collective-permute-start | bytes 56 | tf_op jit(solution)/shard_map/ppermute | solution.py:37
